TPU v7x, 32 devices: a whole 2x2x4 slice. The times are simulated.
32 devices in a mesh: inner: 4 (over x, core), outer: 8 (over z, y).
Axes of the slice: x: 2, y: 2, z: 4, core: 2. Of those that a mesh axis runs over, the one named last changes fastest.
Arguments:
- queries: bfloat16 [4096, 1024], P(('inner', 'outer')), may hold values from -6 to 6
- keys: bfloat16 [4096, 128], P(('inner', 'outer')), may hold values from -6 to 6
- values: bfloat16 [4096, 128], P(('inner', 'outer')), may hold values from -6 to 6
- out_grad: bfloat16 [4096, 1024], P(('inner', 'outer')), may hold values from -6 to 6
- forward_out: bfloat16 [4096, 1024], P(('inner', 'outer')), may hold values from -0.796875 to 0.796875
- log_sum_exp: float32 [8, 4096], P(None, ('inner', 'outer')), may hold values from 3 to 5
- span_table: int32 [64], replicated, may hold values from 0 to 63, each once
- mask_codes: int32 [32, 6], P(('inner', 'outer')), may hold values from 0 to 2
Outputs:
- query_grad: bfloat16 [4096, 1024], P(('inner', 'outer'))
- key_grad: bfloat16 [4096, 128], P(('inner', 'outer'))
- value_grad: bfloat16 [4096, 128], P(('inner', 'outer'))
Inputs may be any that keep to these rules, and one draw needn't show every extreme that they name: `span_table`: each span number appears exactly once.
All inputs are finite; a program needn't handle non-finite values.
Results may differ from a plain program's by a relative error of at most 0.0057.
Values may be sent and summed in bfloat16 or wider, within the bound.
A program may use at most 64 MiB of HBM per device.

v0:
```python
import jax
import jax.numpy as jnp
from jax import lax
from jax.sharding import PartitionSpec as P

WINDOW_PATH = ((0, 0), (1, 0), (2, 0), (2, 1), (3, 1), (4, 1), (4, 2))


def passed_along(block, axis, distance):
    devices = range(lax.axis_size(axis))
    route = [((i - distance) % len(devices), i) for i in devices]
    return lax.ppermute(block, axis, route)


def move_blocks(pair, along):
    if along == "inner":
        return passed_along((pair[0], pair[1]), "inner", 1)
    return passed_along((pair[0], pair[1]), "outer", 1)


def move_sums(pair, along, hop_count):
    if along == "inner":
        return passed_along(pair, "inner", hop_count)
    return passed_along(pair, "outer", hop_count)


def step_along(window_step):
    if WINDOW_PATH[window_step][0] != WINDOW_PATH[window_step - 1][0]:
        return "inner"
    return "outer"


def shards(queries, keys, values, out_grad, forward_out, log_sum_exp, span_table, mask_codes):
    row_count, feature_count = queries.shape
    head_count = log_sum_exp.shape[0]
    head_width = keys.shape[1]
    half_rows = row_count // 2
    score_scale = head_width ** (-0.5)
    inner_count = lax.axis_size("inner")
    outer_count = lax.axis_size("outer")
    inner_at = lax.axis_index("inner")
    outer_at = lax.axis_index("outer")
    span_pairs = span_table.reshape(inner_count * outer_count, 2)
    offsets = jnp.arange(half_rows, dtype=jnp.int32)

    def positions(window_step):
        inner_pos = (inner_at - WINDOW_PATH[window_step][0]) % inner_count
        outer_pos = (outer_at - WINDOW_PATH[window_step][1]) % outer_count
        span_pair = span_pairs[inner_pos * outer_count + outer_pos]
        return (span_pair[:, None] * half_rows + offsets[None, :]).reshape(row_count)

    query_pos = positions(0)
    query_heads = queries.reshape(row_count, head_count, head_width)
    gradient_heads = out_grad.reshape(row_count, head_count, head_width)
    output_heads = forward_out.reshape(row_count, head_count, head_width)
    delta = jnp.einsum(
        "qhd,qhd->hq", gradient_heads, output_heads, preferred_element_type=jnp.float32
    )
    query_sum = jnp.zeros((row_count, feature_count), jnp.float32)
    key_block, value_block = (keys, values)
    carried = None
    for window_step in range(len(WINDOW_PATH)):
        if window_step > 0:
            key_block, value_block = move_blocks((key_block, value_block), step_along(window_step))
            carried = move_sums(carried, step_along(window_step), 1)
        if window_step == 0:
            visit_mask_code = jnp.int32(1)
        else:
            visit_mask_code = mask_codes[0, window_step - 1]
        visit_key_pos = positions(window_step)
        scores = (
            jnp.einsum("qhd,kd->hqk", query_heads, key_block, preferred_element_type=jnp.float32)
            * score_scale
        )
        allowed = (visit_mask_code == 2) | (visit_mask_code == 1) & (
            visit_key_pos[None, :] <= query_pos[:, None]
        )
        probs = jnp.where(allowed[None], jnp.exp(scores - log_sum_exp[:, :, None]), 0.0)
        probs_low = probs.astype(jnp.bfloat16)
        value_part = jnp.einsum(
            "hqk,qhd->kd", probs_low, gradient_heads, preferred_element_type=jnp.float32
        )
        dprob = jnp.einsum(
            "qhd,kd->hqk", gradient_heads, value_block, preferred_element_type=jnp.float32
        )
        dscore = (probs * (dprob - delta[:, :, None]) * score_scale).astype(jnp.bfloat16)
        query_part = jnp.einsum(
            "hqk,kd->qhd", dscore, key_block, preferred_element_type=jnp.float32
        ).reshape(row_count, feature_count)
        key_part = jnp.einsum(
            "hqk,qhd->kd", dscore, query_heads, preferred_element_type=jnp.float32
        )
        query_part, key_part, value_part = (query_part, key_part, value_part)
        query_sum = query_sum + query_part
        if carried is None:
            carried = (key_part, value_part)
        else:
            carried = (carried[0] + key_part, carried[1] + value_part)
    carried = move_sums(carried, "inner", -WINDOW_PATH[-1][0])
    carried = move_sums(carried, "outer", -WINDOW_PATH[-1][1])
    return (
        query_sum.astype(jnp.bfloat16),
        carried[0].astype(jnp.bfloat16),
        carried[1].astype(jnp.bfloat16),
    )


def solution(mesh):
    return jax.shard_map(
        shards,
        mesh=mesh,
        in_specs=(
            P(("inner", "outer"), None),
            P(("inner", "outer"), None),
            P(("inner", "outer"), None),
            P(("inner", "outer"), None),
            P(("inner", "outer"), None),
            P(None, ("inner", "outer")),
            P(),
            P(("inner", "outer"), None),
        ),
        out_specs=(
            P(("inner", "outer"), None),
            P(("inner", "outer"), None),
            P(("inner", "outer"), None),
        ),
        check_vma=False,
    )
```

profile of v0, /device:TPU:0, one launch (start us, length us, event | category | flops | bytes accessed | tf_op | source)
XLA Modules:
  0.0 66.5 jit_solution(3620359525186583575)
XLA Ops:
  1.2 2.6 %collective-permute-start = (bf16[128,128]{1,0:T(8,128)(2,1)}, bf16[128,128]{1,0:T(8,128)(2,1)S(1)}, u32[]{:S(2)}, u32[]{:S(2)}) collective-permute-start(bf16[128,128]{1,0:T(8,128)(2,1)} %param.9), channel_id=1, source_target_pairs={{24,0},{0,8},{8,16},{16,24},{25,1},{1,9},{9,17},{17,25},{26,2},{2,... | collective-permute-start | bytes 98312 | tf_op jit(solution)/shard_map/ppermute | solution.py:12
  3.8 1.5 %fusion.159 = (s32[1,1]{1,0:T(1,128)}, s32[1,1]{1,0:T(1,128)}, s32[1,1]{1,0:T(1,128)}, s32[1,1]{1,0:T(1,128)}, s32[1,1]{1,0:T(1,128)}, /*index=5*/s32[1,1]{1,0:T(1,128)}) fusion(s32[1,6]{1,0:T(1,128)} %param.15), kind=kLoop, calls=%fused_computation.215 | loop fusion | bytes 48 | tf_op jit(solution)/shard_map/slice | solution.py:69
  14.0 0.9 %copy-done.1 = bf16[128,1024]{1,0:T(8,128)(2,1)S(1)} copy-done((bf16[128,1024]{1,0:T(8,128)(2,1)S(1)}, bf16[128,1024]{1,0:T(8,128)(2,1)}, u32[]{:S(2)}) %copy-start.1) | copy-done | bytes 262168
  18.1 2.0 %collective-permute-start.2 = (bf16[128,128]{1,0:T(8,128)(2,1)S(1)}, bf16[128,128]{1,0:T(8,128)(2,1)S(1)}, u32[]{:S(2)}, u32[]{:S(2)}) collective-permute-start(bf16[128,128]{1,0:T(8,128)(2,1)S(1)} %collective-permute-done), channel_id=1, source_target_pairs={{24,0},{0,8},{8,16},{16,24},{25,1},{1,9},{9,17},{17,25},{26,2},{2,... | collective-permute-start | bytes 98312 | tf_op jit(solution)/shard_map/ppermute | solution.py:12
  20.9 1.4 %collective-permute-done.2 = bf16[128,128]{1,0:T(8,128)(2,1)S(1)} collective-permute-done((bf16[128,128]{1,0:T(8,128)(2,1)S(1)}, bf16[128,128]{1,0:T(8,128)(2,1)S(1)}, u32[]{:S(2)}, u32[]{:S(2)}) %collective-permute-start.2) | collective-permute-done | bytes 32800 | tf_op jit(solution)/shard_map/ppermute | solution.py:12
  23.9 1.6 %collective-permute-start.4 = (bf16[128,128]{1,0:T(8,128)(2,1)S(1)}, bf16[128,128]{1,0:T(8,128)(2,1)S(1)}, u32[]{:S(2)}, u32[]{:S(2)}) collective-permute-start(bf16[128,128]{1,0:T(8,128)(2,1)S(1)} %collective-permute-done.2), channel_id=1, source_target_pairs={{7,0},{0,1},{1,2},{2,3},{3,4},{4,5},{5,6},{6,7},{15,8},{8,9},{9,10... | collective-permute-start | bytes 98312 | tf_op jit(solution)/shard_map/ppermute | solution.py:12
  25.7 1.2 %collective-permute-start.21 = (f32[128,128]{1,0:T(8,128)S(1)}, f32[128,128]{1,0:T(8,128)S(1)}, u32[]{:S(2)}, u32[]{:S(2)}) collective-permute-start(f32[128,128]{1,0:T(8,128)S(1)} %fusion.58), channel_id=1, source_target_pairs={{24,0},{0,8},{8,16},{16,24},{25,1},{1,9},{9,17},{17,25},{26,2},{2,... | collective-permute-start | bytes 196616 | tf_op jit(solution)/shard_map/ppermute | solution.py:12
  26.9 1.5 %collective-permute-start.5 = (bf16[128,128]{1,0:T(8,128)(2,1)S(1)}, bf16[128,128]{1,0:T(8,128)(2,1)S(1)}, u32[]{:S(2)}, u32[]{:S(2)}) collective-permute-start(bf16[128,128]{1,0:T(8,128)(2,1)S(1)} %collective-permute-done.3), channel_id=1, source_target_pairs={{7,0},{0,1},{1,2},{2,3},{3,4},{4,5},{5,6},{6,7},{15,8},{8,9},{9,10... | collective-permute-start | bytes 98312 | tf_op jit(solution)/shard_map/ppermute | solution.py:12
  28.4 2.2 %collective-permute-done.4 = bf16[128,128]{1,0:T(8,128)(2,1)S(1)} collective-permute-done((bf16[128,128]{1,0:T(8,128)(2,1)S(1)}, bf16[128,128]{1,0:T(8,128)(2,1)S(1)}, u32[]{:S(2)}, u32[]{:S(2)}) %collective-permute-start.4) | collective-permute-done | bytes 32800 | tf_op jit(solution)/shard_map/ppermute | solution.py:12
  31.5 2.0 %collective-permute-done.5 = bf16[128,128]{1,0:T(8,128)(2,1)S(1)} collective-permute-done((bf16[128,128]{1,0:T(8,128)(2,1)S(1)}, bf16[128,128]{1,0:T(8,128)(2,1)S(1)}, u32[]{:S(2)}, u32[]{:S(2)}) %collective-permute-start.5) | collective-permute-done | bytes 32800 | tf_op jit(solution)/shard_map/ppermute | solution.py:12
  35.1 0.6 collective-permute-start.8
  35.7 1.1 %collective-permute-done.7 = bf16[128,128]{1,0:T(8,128)(2,1)S(1)} collective-permute-done((bf16[128,128]{1,0:T(8,128)(2,1)S(1)}, bf16[128,128]{1,0:T(8,128)(2,1)S(1)}, u32[]{:S(2)}, u32[]{:S(2)}) %collective-permute-start.7) | collective-permute-done | bytes 32800 | tf_op jit(solution)/shard_map/ppermute | solution.py:12
  37.6 1.1 %collective-permute-start.14 = (f32[128,128]{1,0:T(8,128)S(1)}, f32[128,128]{1,0:T(8,128)S(1)}, u32[]{:S(2)}, u32[]{:S(2)}) collective-permute-start(f32[128,128]{1,0:T(8,128)S(1)} %add.358), channel_id=1, source_target_pairs={{7,0},{0,1},{1,2},{2,3},{3,4},{4,5},{5,6},{6,7},{15,8},{8,9},{9,10... | collective-permute-start | bytes 196616 | tf_op jit(solution)/shard_map/ppermute | solution.py:12
  39.2 1.0 %collective-permute-start.10 = (bf16[128,128]{1,0:T(8,128)(2,1)S(1)}, bf16[128,128]{1,0:T(8,128)(2,1)S(1)}, u32[]{:S(2)}, u32[]{:S(2)}) collective-permute-start(bf16[128,128]{1,0:T(8,128)(2,1)S(1)} %collective-permute-done.8), channel_id=1, source_target_pairs={{7,0},{0,1},{1,2},{2,3},{3,4},{4,5},{5,6},{6,7},{15,8},{8,9},{9,10... | collective-permute-start | bytes 98312 | tf_op jit(solution)/shard_map/ppermute | solution.py:12
  40.7 2.2 %collective-permute-start.11 = (bf16[128,128]{1,0:T(8,128)(2,1)S(1)}, bf16[128,128]{1,0:T(8,128)(2,1)S(1)}, u32[]{:S(2)}, u32[]{:S(2)}) collective-permute-start(bf16[128,128]{1,0:T(8,128)(2,1)S(1)} %collective-permute-done.9), channel_id=1, source_target_pairs={{7,0},{0,1},{1,2},{2,3},{3,4},{4,5},{5,6},{6,7},{15,8},{8,9},{9,10... | collective-permute-start | bytes 98312 | tf_op jit(solution)/shard_map/ppermute | solution.py:12
  42.8 2.5 %collective-permute-done.14 = f32[128,128]{1,0:T(8,128)S(1)} collective-permute-done((f32[128,128]{1,0:T(8,128)S(1)}, f32[128,128]{1,0:T(8,128)S(1)}, u32[]{:S(2)}, u32[]{:S(2)}) %collective-permute-start.14) | collective-permute-done | bytes 65568 | tf_op jit(solution)/shard_map/ppermute | solution.py:12
  46.5 0.8 %collective-permute-done.11 = bf16[128,128]{1,0:T(8,128)(2,1)S(1)} collective-permute-done((bf16[128,128]{1,0:T(8,128)(2,1)S(1)}, bf16[128,128]{1,0:T(8,128)(2,1)S(1)}, u32[]{:S(2)}, u32[]{:S(2)}) %collective-permute-start.11) | collective-permute-done | bytes 32800 | tf_op jit(solution)/shard_map/ppermute | solution.py:12
  47.6 1.5 %collective-permute-done.15 = f32[128,128]{1,0:T(8,128)S(1)} collective-permute-done((f32[128,128]{1,0:T(8,128)S(1)}, f32[128,128]{1,0:T(8,128)S(1)}, u32[]{:S(2)}, u32[]{:S(2)}) %collective-permute-start.15) | collective-permute-done | bytes 65568 | tf_op jit(solution)/shard_map/ppermute | solution.py:12
  49.2 0.6 collective-permute-done.23
  50.1 2.7 %collective-permute-done.16 = f32[128,128]{1,0:T(8,128)S(1)} collective-permute-done((f32[128,128]{1,0:T(8,128)S(1)}, f32[128,128]{1,0:T(8,128)S(1)}, u32[]{:S(2)}, u32[]{:S(2)}) %collective-permute-start.16) | collective-permute-done | bytes 65568 | tf_op jit(solution)/shard_map/ppermute | solution.py:12
  53.9 6.1 %collective-permute-done.17 = f32[128,128]{1,0:T(8,128)S(1)} collective-permute-done((f32[128,128]{1,0:T(8,128)S(1)}, f32[128,128]{1,0:T(8,128)S(1)}, u32[]{:S(2)}, u32[]{:S(2)}) %collective-permute-start.17) | collective-permute-done | bytes 65568 | tf_op jit(solution)/shard_map/ppermute | solution.py:12
  60.0 0.7 %collective-permute-done.25 = f32[128,128]{1,0:T(8,128)S(1)} collective-permute-done((f32[128,128]{1,0:T(8,128)S(1)}, f32[128,128]{1,0:T(8,128)S(1)}, u32[]{:S(2)}, u32[]{:S(2)}) %collective-permute-start.25) | collective-permute-done | bytes 65568 | tf_op jit(solution)/shard_map/ppermute | solution.py:12
  61.7 0.9 %copy.96 = bf16[128,1024]{1,0:T(8,128)(2,1)} copy(bf16[128,1024]{0,1:T(8,128)(2,1)S(1)} %bitcast.419) | data formatting | bytes 524288
  62.6 2.4 %collective-permute-done.19 = bf16[128,128]{1,0:T(8,128)(2,1)S(1)} collective-permute-done((bf16[128,128]{1,0:T(8,128)(2,1)S(1)}, bf16[128,128]{1,0:T(8,128)(2,1)S(1)}, u32[]{:S(2)}, u32[]{:S(2)}) %collective-permute-start.19) | collective-permute-done | bytes 32800 | tf_op jit(solution)/shard_map/ppermute | solution.py:12
  (113 shorter events, 16.6 us)
Async XLA Ops:
  0.7 17.4 %collective-permute-start.1 = (bf16[128,128]{1,0:T(8,128)(2,1)}, bf16[128,128]{1,0:T(8,128)(2,1)S(1)}, u32[]{:S(2)}, u32[]{:S(2)}) collective-permute-start(bf16[128,128]{1,0:T(8,128)(2,1)} %param.10), channel_id=1, source_target_pairs={{24,0},{0,8},{8,16},{16,24},{25,1},{1,9},{9,17},{17,25},{26,2},{2,... | collective-permute-start | bytes 98312 | tf_op jit(solution)/shard_map/ppermute | solution.py:12
  1.2 16.9 %collective-permute-start = (bf16[128,128]{1,0:T(8,128)(2,1)}, bf16[128,128]{1,0:T(8,128)(2,1)S(1)}, u32[]{:S(2)}, u32[]{:S(2)}) collective-permute-start(bf16[128,128]{1,0:T(8,128)(2,1)} %param.9), channel_id=1, source_target_pairs={{24,0},{0,8},{8,16},{16,24},{25,1},{1,9},{9,17},{17,25},{26,2},{2,... | collective-permute-start | bytes 98312 | tf_op jit(solution)/shard_map/ppermute | solution.py:12
  17.2 5.9 %collective-permute-start.12 = (f32[128,128]{1,0:T(8,128)S(1)}, f32[128,128]{1,0:T(8,128)S(1)}, u32[]{:S(2)}, u32[]{:S(2)}) collective-permute-start(f32[128,128]{1,0:T(8,128)S(1)} %convolution_bitcast_fusion.20), channel_id=1, source_target_pairs={{24,0},{0,8},{8,16},{16,24},{25,1},{1,9},{9,17},{17,25},{26,2},{2,... | collective-permute-start | bytes 196616 | tf_op jit(solution)/shard_map/ppermute | solution.py:12
  17.6 7.9 %collective-permute-start.20 = (f32[128,128]{1,0:T(8,128)S(1)}, f32[128,128]{1,0:T(8,128)S(1)}, u32[]{:S(2)}, u32[]{:S(2)}) collective-permute-start(f32[128,128]{1,0:T(8,128)S(1)} %convolution_bitcast_fusion.13), channel_id=1, source_target_pairs={{24,0},{0,8},{8,16},{16,24},{25,1},{1,9},{9,17},{17,25},{26,2},{2,... | collective-permute-start | bytes 196616 | tf_op jit(solution)/shard_map/ppermute | solution.py:12
  18.0 4.6 %collective-permute-start.3 = (bf16[128,128]{1,0:T(8,128)(2,1)S(1)}, bf16[128,128]{1,0:T(8,128)(2,1)S(1)}, u32[]{:S(2)}, u32[]{:S(2)}) collective-permute-start(bf16[128,128]{1,0:T(8,128)(2,1)S(1)} %collective-permute-done.1), channel_id=1, source_target_pairs={{24,0},{0,8},{8,16},{16,24},{25,1},{1,9},{9,17},{17,25},{26,2},{2,... | collective-permute-start | bytes 98312 | tf_op jit(solution)/shard_map/ppermute | solution.py:12
  18.1 4.2 %collective-permute-start.2 = (bf16[128,128]{1,0:T(8,128)(2,1)S(1)}, bf16[128,128]{1,0:T(8,128)(2,1)S(1)}, u32[]{:S(2)}, u32[]{:S(2)}) collective-permute-start(bf16[128,128]{1,0:T(8,128)(2,1)S(1)} %collective-permute-done), channel_id=1, source_target_pairs={{24,0},{0,8},{8,16},{16,24},{25,1},{1,9},{9,17},{17,25},{26,2},{2,... | collective-permute-start | bytes 98312 | tf_op jit(solution)/shard_map/ppermute | solution.py:12
  23.9 13.8 %collective-permute-start.13 = (f32[128,128]{1,0:T(8,128)S(1)}, f32[128,128]{1,0:T(8,128)S(1)}, u32[]{:S(2)}, u32[]{:S(2)}) collective-permute-start(f32[128,128]{1,0:T(8,128)S(1)} %fusion.57), channel_id=1, source_target_pairs={{24,0},{0,8},{8,16},{16,24},{25,1},{1,9},{9,17},{17,25},{26,2},{2,... | collective-permute-start | bytes 196616 | tf_op jit(solution)/shard_map/ppermute | solution.py:12
  23.9 6.7 %collective-permute-start.4 = (bf16[128,128]{1,0:T(8,128)(2,1)S(1)}, bf16[128,128]{1,0:T(8,128)(2,1)S(1)}, u32[]{:S(2)}, u32[]{:S(2)}) collective-permute-start(bf16[128,128]{1,0:T(8,128)(2,1)S(1)} %collective-permute-done.2), channel_id=1, source_target_pairs={{7,0},{0,1},{1,2},{2,3},{3,4},{4,5},{5,6},{6,7},{15,8},{8,9},{9,10... | collective-permute-start | bytes 98312 | tf_op jit(solution)/shard_map/ppermute | solution.py:12
  25.7 9.2 %collective-permute-start.21 = (f32[128,128]{1,0:T(8,128)S(1)}, f32[128,128]{1,0:T(8,128)S(1)}, u32[]{:S(2)}, u32[]{:S(2)}) collective-permute-start(f32[128,128]{1,0:T(8,128)S(1)} %fusion.58), channel_id=1, source_target_pairs={{24,0},{0,8},{8,16},{16,24},{25,1},{1,9},{9,17},{17,25},{26,2},{2,... | collective-permute-start | bytes 196616 | tf_op jit(solution)/shard_map/ppermute | solution.py:12
  26.9 6.6 %collective-permute-start.5 = (bf16[128,128]{1,0:T(8,128)(2,1)S(1)}, bf16[128,128]{1,0:T(8,128)(2,1)S(1)}, u32[]{:S(2)}, u32[]{:S(2)}) collective-permute-start(bf16[128,128]{1,0:T(8,128)(2,1)S(1)} %collective-permute-done.3), channel_id=1, source_target_pairs={{7,0},{0,1},{1,2},{2,3},{3,4},{4,5},{5,6},{6,7},{15,8},{8,9},{9,10... | collective-permute-start | bytes 98312 | tf_op jit(solution)/shard_map/ppermute | solution.py:12
  31.1 3.4 %collective-permute-start.6 = (bf16[128,128]{1,0:T(8,128)(2,1)S(1)}, bf16[128,128]{1,0:T(8,128)(2,1)S(1)}, u32[]{:S(2)}, u32[]{:S(2)}) collective-permute-start(bf16[128,128]{1,0:T(8,128)(2,1)S(1)} %collective-permute-done.4), channel_id=1, source_target_pairs={{24,0},{0,8},{8,16},{16,24},{25,1},{1,9},{9,17},{17,25},{26,2},{2,... | collective-permute-start | bytes 98312 | tf_op jit(solution)/shard_map/ppermute | solution.py:12
  35.0 10.4 %collective-permute-start.22 = (f32[128,128]{1,0:T(8,128)S(1)}, f32[128,128]{1,0:T(8,128)S(1)}, u32[]{:S(2)}, u32[]{:S(2)}) collective-permute-start(f32[128,128]{1,0:T(8,128)S(1)} %add.364), channel_id=1, source_target_pairs={{7,0},{0,1},{1,2},{2,3},{3,4},{4,5},{5,6},{6,7},{15,8},{8,9},{9,10... | collective-permute-start | bytes 196616 | tf_op jit(solution)/shard_map/ppermute | solution.py:12
  35.1 3.6 %collective-permute-start.8 = (bf16[128,128]{1,0:T(8,128)(2,1)S(1)}, bf16[128,128]{1,0:T(8,128)(2,1)S(1)}, u32[]{:S(2)}, u32[]{:S(2)}) collective-permute-start(bf16[128,128]{1,0:T(8,128)(2,1)S(1)} %collective-permute-done.6), channel_id=1, source_target_pairs={{24,0},{0,8},{8,16},{16,24},{25,1},{1,9},{9,17},{17,25},{26,2},{2,... | collective-permute-start | bytes 98312 | tf_op jit(solution)/shard_map/ppermute | solution.py:12
  37.6 7.7 %collective-permute-start.14 = (f32[128,128]{1,0:T(8,128)S(1)}, f32[128,128]{1,0:T(8,128)S(1)}, u32[]{:S(2)}, u32[]{:S(2)}) collective-permute-start(f32[128,128]{1,0:T(8,128)S(1)} %add.358), channel_id=1, source_target_pairs={{7,0},{0,1},{1,2},{2,3},{3,4},{4,5},{5,6},{6,7},{15,8},{8,9},{9,10... | collective-permute-start | bytes 196616 | tf_op jit(solution)/shard_map/ppermute | solution.py:12
  39.2 7.0 %collective-permute-start.10 = (bf16[128,128]{1,0:T(8,128)(2,1)S(1)}, bf16[128,128]{1,0:T(8,128)(2,1)S(1)}, u32[]{:S(2)}, u32[]{:S(2)}) collective-permute-start(bf16[128,128]{1,0:T(8,128)(2,1)S(1)} %collective-permute-done.8), channel_id=1, source_target_pairs={{7,0},{0,1},{1,2},{2,3},{3,4},{4,5},{5,6},{6,7},{15,8},{8,9},{9,10... | collective-permute-start | bytes 98312 | tf_op jit(solution)/shard_map/ppermute | solution.py:12
  40.7 6.7 %collective-permute-start.11 = (bf16[128,128]{1,0:T(8,128)(2,1)S(1)}, bf16[128,128]{1,0:T(8,128)(2,1)S(1)}, u32[]{:S(2)}, u32[]{:S(2)}) collective-permute-start(bf16[128,128]{1,0:T(8,128)(2,1)S(1)} %collective-permute-done.9), channel_id=1, source_target_pairs={{7,0},{0,1},{1,2},{2,3},{3,4},{4,5},{5,6},{6,7},{15,8},{8,9},{9,10... | collective-permute-start | bytes 98312 | tf_op jit(solution)/shard_map/ppermute | solution.py:12
  45.4 3.7 %collective-permute-start.15 = (f32[128,128]{1,0:T(8,128)S(1)}, f32[128,128]{1,0:T(8,128)S(1)}, u32[]{:S(2)}, u32[]{:S(2)}) collective-permute-start(f32[128,128]{1,0:T(8,128)S(1)} %add.359), channel_id=1, source_target_pairs={{24,0},{0,8},{8,16},{16,24},{25,1},{1,9},{9,17},{17,25},{26,2},{2,... | collective-permute-start | bytes 196616 | tf_op jit(solution)/shard_map/ppermute | solution.py:12
  45.5 4.4 %collective-permute-start.23 = (f32[128,128]{1,0:T(8,128)S(1)}, f32[128,128]{1,0:T(8,128)S(1)}, u32[]{:S(2)}, u32[]{:S(2)}) collective-permute-start(f32[128,128]{1,0:T(8,128)S(1)} %add.365), channel_id=1, source_target_pairs={{24,0},{0,8},{8,16},{16,24},{25,1},{1,9},{9,17},{17,25},{26,2},{2,... | collective-permute-start | bytes 196616 | tf_op jit(solution)/shard_map/ppermute | solution.py:12
  49.1 3.7 %collective-permute-start.16 = (f32[128,128]{1,0:T(8,128)S(1)}, f32[128,128]{1,0:T(8,128)S(1)}, u32[]{:S(2)}, u32[]{:S(2)}) collective-permute-start(f32[128,128]{1,0:T(8,128)S(1)} %add.360), channel_id=1, source_target_pairs={{24,0},{0,8},{8,16},{16,24},{25,1},{1,9},{9,17},{17,25},{26,2},{2,... | collective-permute-start | bytes 196616 | tf_op jit(solution)/shard_map/ppermute | solution.py:12
  49.8 3.7 %collective-permute-start.24 = (f32[128,128]{1,0:T(8,128)S(1)}, f32[128,128]{1,0:T(8,128)S(1)}, u32[]{:S(2)}, u32[]{:S(2)}) collective-permute-start(f32[128,128]{1,0:T(8,128)S(1)} %add.366), channel_id=1, source_target_pairs={{24,0},{0,8},{8,16},{16,24},{25,1},{1,9},{9,17},{17,25},{26,2},{2,... | collective-permute-start | bytes 196616 | tf_op jit(solution)/shard_map/ppermute | solution.py:12
  52.9 7.1 %collective-permute-start.17 = (f32[128,128]{1,0:T(8,128)S(1)}, f32[128,128]{1,0:T(8,128)S(1)}, u32[]{:S(2)}, u32[]{:S(2)}) collective-permute-start(f32[128,128]{1,0:T(8,128)S(1)} %add.361), channel_id=1, source_target_pairs={{7,0},{0,1},{1,2},{2,3},{3,4},{4,5},{5,6},{6,7},{15,8},{8,9},{9,10... | collective-permute-start | bytes 196616 | tf_op jit(solution)/shard_map/ppermute | solution.py:12
  53.6 7.1 %collective-permute-start.25 = (f32[128,128]{1,0:T(8,128)S(1)}, f32[128,128]{1,0:T(8,128)S(1)}, u32[]{:S(2)}, u32[]{:S(2)}) collective-permute-start(f32[128,128]{1,0:T(8,128)S(1)} %add.367), channel_id=1, source_target_pairs={{7,0},{0,1},{1,2},{2,3},{3,4},{4,5},{5,6},{6,7},{15,8},{8,9},{9,10... | collective-permute-start | bytes 196616 | tf_op jit(solution)/shard_map/ppermute | solution.py:12
  61.0 4.0 %collective-permute-start.19 = (bf16[128,128]{1,0:T(8,128)(2,1)S(1)}, bf16[128,128]{1,0:T(8,128)(2,1)S(1)}, u32[]{:S(2)}, u32[]{:S(2)}) collective-permute-start(bf16[128,128]{1,0:T(8,128)(2,1)S(1)} %collective-permute-done.18), channel_id=1, source_target_pairs={{2,0},{3,1},{4,2},{5,3},{6,4},{7,5},{0,6},{1,7},{10,8},{11,9},{12,... | collective-permute-start | bytes 98312 | tf_op jit(solution)/shard_map/ppermute | solution.py:12
  61.1 4.2 %collective-permute-start.27 = (bf16[128,128]{1,0:T(8,128)(2,1)S(1)}, bf16[128,128]{1,0:T(8,128)(2,1)S(1)}, u32[]{:S(2)}, u32[]{:S(2)}) collective-permute-start(bf16[128,128]{1,0:T(8,128)(2,1)S(1)} %collective-permute-done.26), channel_id=1, source_target_pairs={{2,0},{3,1},{4,2},{5,3},{6,4},{7,5},{0,6},{1,7},{10,8},{11,9},{12,... | collective-permute-start | bytes 98312 | tf_op jit(solution)/shard_map/ppermute | solution.py:12
  (11 other events, 40.1 us)
where the time goes:
time: 66.9 us; the launch traced here: 66.5 us
  waiting for transfers between devices  25.8 us (39%)
  starting transfers between devices  16.3 us (24%)
  between operations  8.8 us (13%)
  matrix products  8.45 us (13%)
  local copies, waits for them, and re-layouts  6.36 us (10%)
  other arithmetic  0.83 us (1%)
    ppermute x28, waiting for transfers between devices, passed_along(): return lax.ppermute(block, axis, route)  25.8 us
    ppermute x28, starting transfers between devices, passed_along(): return lax.ppermute(block, axis, route)  16.3 us
    unnamed x19, local copies, waits for them, and re-layouts  4.14 us
    dot_general x7, matrix products, shards(): jnp.einsum('hqk,kd->qhd', dscore, key_block, preferred_element_type=jnp.f...  1.86 us
    dot_general x7, matrix products, shards(): jnp.einsum('qhd,kd->hqk', query_heads, key_block, preferred_element_type=...  1.81 us
    dot_general x7, matrix products, shards(): jnp.einsum('qhd,kd->hqk', gradient_heads, value_block, preferred_element_...  1.65 us
    dot_general x7, matrix products, shards(): jnp.einsum('hqk,qhd->kd', probs_low, gradient_heads, preferred_element_ty...  1.57 us
    dot_general x7, matrix products, shards(): jnp.einsum('hqk,qhd->kd', dscore, query_heads, preferred_element_type=jnp...  1.56 us
  transfers between devices with their start and end apart: 28, of which 16 were waited for; matrix products, arithmetic and copies ran while one was open for 19% of the time, Pallas kernels for 0%

commit v1 on v0

v1 whole, which is shorter than its diff:
```python
import functools

import jax
import jax.numpy as jnp
from jax import lax
from jax.experimental import pallas as pl
from jax.experimental.pallas import tpu as pltpu
from jax.sharding import PartitionSpec as P

WINDOW_PATH = ((0, 0), (1, 0), (2, 0), (2, 1), (3, 1), (4, 1), (4, 2))
STEP_ORDER = (1, 2, 5, 4, 3, 6)
MESH = pl.DeviceIdType.MESH


def kernel(inner_count, outer_count, q_hbm, k_hbm, v_hbm, do_hbm, o_hbm, lse_ref, span_ref, code_ref,
           dq_ref, dk_ref, dv_ref,
           q_vm, do_vm, o_vm, kv_own, kv_in, g_out, g_in, dq_acc, own_acc,
           load_sem, kv_send, kv_recv, g_send, g_recv):
    inner_at = lax.axis_index("inner")
    outer_at = lax.axis_index("outer")
    head_count, rows, width = q_vm.shape
    half = rows // 2
    scale = width ** (-0.5)
    steps = range(1, len(WINDOW_PATH))

    def device(step, sign):
        a, c = WINDOW_PATH[step]
        u = lax.rem(inner_at + (sign * a) % inner_count, inner_count)
        w = lax.rem(outer_at + (sign * c) % outer_count, outer_count)
        return u, w

    barrier = pltpu.get_barrier_semaphore()
    for step in steps:
        for sign in (1, -1):
            pl.semaphore_signal(barrier, inc=1, device_id=device(step, sign), device_id_type=MESH)

    loads = []

    def load(src, dst, slot):
        copy = pltpu.make_async_copy(src, dst, load_sem.at[slot])
        copy.start()
        loads.append(copy)

    load(k_hbm, kv_own.at[0], 0)
    load(v_hbm, kv_own.at[1], 1)
    for h in range(head_count):
        columns = pl.ds(h * width, width)
        load(q_hbm.at[:, columns], q_vm.at[h], 2 + 3 * h)
        load(do_hbm.at[:, columns], do_vm.at[h], 3 + 3 * h)
        load(o_hbm.at[:, columns], o_vm.at[h], 4 + 3 * h)
    for copy in loads:
        copy.wait()

    pl.semaphore_wait(barrier, 2 * len(steps))

    def kv_copy(step):
        return pltpu.make_async_remote_copy(
            src_ref=kv_own, dst_ref=kv_in.at[step - 1],
            send_sem=kv_send.at[step - 1], recv_sem=kv_recv.at[step - 1],
            device_id=device(step, 1), device_id_type=MESH)

    def g_copy(step):
        return pltpu.make_async_remote_copy(
            src_ref=g_out.at[step - 1], dst_ref=g_in.at[step - 1],
            send_sem=g_send.at[step - 1], recv_sem=g_recv.at[step - 1],
            device_id=device(step, -1), device_id_type=MESH)

    for step in STEP_ORDER:
        kv_copy(step).start()

    def spans(step):
        u, w = device(step, -1)
        block = u * outer_count + w
        return span_ref[2 * block], span_ref[2 * block + 1]

    def position(step, dim):
        first, second = spans(step)
        at = lax.broadcasted_iota(jnp.int32, (rows, rows), dim)
        return jnp.where(at < half, first * half + at, second * half + at - half)

    query_pos = position(0, 1)
    lse_row = jnp.concatenate([lse_ref[h:h + 1, :] for h in range(head_count)], axis=1)
    delta_rows = []
    for h in range(head_count):
        product = do_vm[h].astype(jnp.float32) * o_vm[h].astype(jnp.float32)
        delta_rows.append(jnp.sum(product.T, axis=0, keepdims=True))
    delta_row = jnp.concatenate(delta_rows, axis=1)
    features = head_count * rows

    def dot(x, y, dims):
        return lax.dot_general(x, y, (dims, ((), ())), preferred_element_type=jnp.float32)

    def visit(step, key_block, value_block):
        q_all = q_vm[...].reshape(features, width)
        do_all = do_vm[...].reshape(features, width)
        if step == 0:
            allowed = position(0, 0) <= query_pos
        else:
            code = code_ref[0, step - 1]
            limit = jnp.where(code == 2, jnp.int32(2 ** 31 - 1), jnp.int32(-1))
            reach = jnp.where(code == 1, query_pos, limit)
            allowed = position(step, 0) <= reach
        allowed = jnp.concatenate([allowed] * head_count, axis=1)
        scores = dot(key_block, q_all, ((1,), (1,))) * scale
        probs = jnp.where(allowed, jnp.exp(scores - lse_row), 0.0)
        dprob = dot(value_block, do_all, ((1,), (1,)))
        dscore = (probs * (dprob - delta_row) * scale).astype(jnp.bfloat16)
        value_part = dot(probs.astype(jnp.bfloat16), do_all, ((1,), (0,)))
        key_part = dot(dscore, q_all, ((1,), (0,)))
        query_part = dot(key_block.T, dscore, ((1,), (0,)))
        return query_part, key_part, value_part

    dq_acc[...], own_acc[0], own_acc[1] = visit(0, kv_own[0], kv_own[1])
    for step in STEP_ORDER:
        kv_copy(step).wait_recv()
        query_part, key_part, value_part = visit(step, kv_in[step - 1, 0], kv_in[step - 1, 1])
        g_out[step - 1, 0] = key_part.astype(jnp.bfloat16)
        g_out[step - 1, 1] = value_part.astype(jnp.bfloat16)
        g_copy(step).start()
        dq_acc[...] += query_part
    for h in range(head_count):
        columns = pl.ds(h * rows, rows)
        dq_ref[:, pl.ds(h * width, width)] = dq_acc[:, columns].T.astype(jnp.bfloat16)
    total = own_acc[...]
    for step in STEP_ORDER:
        g_copy(step).wait_recv()
        total = total + g_in[step - 1].astype(jnp.float32)
    dk_ref[...] = total[0].astype(jnp.bfloat16)
    dv_ref[...] = total[1].astype(jnp.bfloat16)
    for step in STEP_ORDER:
        kv_copy(step).wait_send()
        g_copy(step).wait_send()


def shards(queries, keys, values, out_grad, forward_out, log_sum_exp, span_table, mask_codes):
    rows, features = queries.shape
    width = keys.shape[1]
    heads = log_sum_exp.shape[0]
    remote = len(WINDOW_PATH) - 1
    hbm = pl.BlockSpec(memory_space=pl.ANY)
    vmem = pl.BlockSpec(memory_space=pltpu.VMEM)
    smem = pl.BlockSpec(memory_space=pltpu.SMEM)
    return pl.pallas_call(
        functools.partial(kernel, lax.axis_size("inner"), lax.axis_size("outer")),
        out_shape=(
            jax.ShapeDtypeStruct((rows, features), jnp.bfloat16),
            jax.ShapeDtypeStruct((rows, width), jnp.bfloat16),
            jax.ShapeDtypeStruct((rows, width), jnp.bfloat16),
        ),
        in_specs=[hbm, hbm, hbm, hbm, hbm, vmem, smem, smem],
        out_specs=(vmem, vmem, vmem),
        scratch_shapes=[
            pltpu.VMEM((heads, rows, width), jnp.bfloat16),
            pltpu.VMEM((heads, rows, width), jnp.bfloat16),
            pltpu.VMEM((heads, rows, width), jnp.bfloat16),
            pltpu.VMEM((2, rows, width), jnp.bfloat16),
            pltpu.VMEM((remote, 2, rows, width), jnp.bfloat16),
            pltpu.VMEM((remote, 2, rows, width), jnp.bfloat16),
            pltpu.VMEM((remote, 2, rows, width), jnp.bfloat16),
            pltpu.VMEM((width, heads * rows), jnp.float32),
            pltpu.VMEM((2, rows, width), jnp.float32),
            pltpu.SemaphoreType.DMA((2 + 3 * heads,)),
            pltpu.SemaphoreType.DMA((remote,)),
            pltpu.SemaphoreType.DMA((remote,)),
            pltpu.SemaphoreType.DMA((remote,)),
            pltpu.SemaphoreType.DMA((remote,)),
        ],
        compiler_params=pltpu.CompilerParams(collective_id=0, has_side_effects=True),
    )(queries, keys, values, out_grad, forward_out, log_sum_exp, span_table, mask_codes)


def solution(mesh):
    return jax.shard_map(
        shards,
        mesh=mesh,
        in_specs=(
            P(("inner", "outer"), None),
            P(("inner", "outer"), None),
            P(("inner", "outer"), None),
            P(("inner", "outer"), None),
            P(("inner", "outer"), None),
            P(None, ("inner", "outer")),
            P(),
            P(("inner", "outer"), None),
        ),
        out_specs=(
            P(("inner", "outer"), None),
            P(("inner", "outer"), None),
            P(("inner", "outer"), None),
        ),
        check_vma=False,
    )
```

time: 66.9 us -> 25 us (0.37)
  waiting for transfers between devices: 25.8 us -> 0 us
  Pallas kernels: 0 us -> 21 us
  starting transfers between devices: 16.3 us -> 0 us
  matrix products: 8.45 us -> 0 us
  between operations: 8.8 us -> 0.65 us
  local copies, waits for them, and re-layouts: 6.36 us -> 3.06 us
  other arithmetic: 0.83 us -> 0 us
    ppermute x28 -> x0, waiting for transfers between devices: 25.8 us -> none  [passed_along(): return lax.ppermute(block, axis, route)]
    pallas_call x0 -> x1, Pallas kernels: none -> 21 us  [shards(): pl.pallas_call(functools.partial(kernel, lax.axis_size('inner'), lax.axis...]
    ppermute x28 -> x0, starting transfers between devices: 16.3 us -> none  [passed_along(): return lax.ppermute(block, axis, route)]
    dot_general x35 -> x0, matrix products: 8.45 us -> none  [the longest x7 1.86 us: shards(): jnp.einsum('hqk,kd->qhd', dscore, key_block, preferred_element_type=jnp.f...]
    slice x1 -> x0, local copies, waits for them, and re-layouts: 1.51 us -> none  [shards(): visit_mask_code = mask_codes[0, window_step - 1]]
    unnamed x19 -> x7, local copies, waits for them, and re-layouts: 4.14 us -> 3.06 us
  transfers between devices with their start and end apart: 28 -> 0, of which waited for: 16 -> 0; matrix products, arithmetic and copies ran while one was open for 19% -> 0% of each run, Pallas kernels for 0% -> 0%
where the time goes in v1:
time: 25 us; the launch traced here: 24.7 us
  Pallas kernels  21 us (84%)
  local copies, waits for them, and re-layouts  3.06 us (12%)
  between operations  0.65 us (3%)
    pallas_call x1, Pallas kernels, shards(): pl.pallas_call(functools.partial(kernel, lax.axis_size('inner'), lax.axis...  21 us
    unnamed x7, local copies, waits for them, and re-layouts  3.06 us

profile of v1, /device:TPU:0, one launch (start us, length us, event | category | flops | bytes accessed | tf_op | source)
XLA Modules:
  0.0 24.7 jit_solution(1513590335122422960)
XLA Ops:
  0.6 21.0 %shard_map.103 = (bf16[128,1024]{1,0:T(8,128)(2,1)}, bf16[128,128]{1,0:T(8,128)(2,1)}, bf16[128,128]{1,0:T(8,128)(2,1)}) custom-call(bf16[128,1024]{1,0:T(8,128)(2,1)} %q_hbm.1, bf16[128,128]{1,0:T(8,128)(2,1)} %k_hbm.1, bf16[128,128]{1,0:T(8,128)(2,1)} %v_hbm.1, bf16[128,1024]{1,0:T(8,128)(2,1)} %do_hbm.1, bf16[128,1024]{1,0:T(8,128)(2,1)} %o_hbm.1, ...), custom_call_target="tpu_custom_call" | custom-call | tf_op jit(solution)/shard_map/pallas_call | solution.py:143
  21.6 0.0 copy-start.1
  21.6 1.7 %copy.14 = bf16[128,1024]{1,0:T(8,128)(2,1)} copy(bf16[128,1024]{1,0:T(8,128)(2,1)} %get-tuple-element.6) | data formatting | bytes 524288
  23.3 0.0 copy-done.1
  23.3 0.0 copy-start
  23.3 0.6 %copy.15 = bf16[128,128]{1,0:T(8,128)(2,1)} copy(bf16[128,128]{1,0:T(8,128)(2,1)S(1)} %copy-done.1) | data formatting | bytes 65536
  23.9 0.2 copy-done
  24.1 0.6 %copy.16 = bf16[128,128]{1,0:T(8,128)(2,1)} copy(bf16[128,128]{1,0:T(8,128)(2,1)S(1)} %copy-done) | data formatting | bytes 65536
Async XLA Ops:
  21.6 1.7 %copy-start.1 = (bf16[128,128]{1,0:T(8,128)(2,1)S(1)}, bf16[128,128]{1,0:T(8,128)(2,1)}, u32[]{:S(2)}) copy-start(bf16[128,128]{1,0:T(8,128)(2,1)} %get-tuple-element.7) | copy-start | bytes 98308
  23.3 0.8 %copy-start = (bf16[128,128]{1,0:T(8,128)(2,1)S(1)}, bf16[128,128]{1,0:T(8,128)(2,1)}, u32[]{:S(2)}) copy-start(bf16[128,128]{1,0:T(8,128)(2,1)} %get-tuple-element.8) | copy-start | bytes 98308

commit v2 on v1

--- a/solution.py
+++ b/solution.py
@@ -9,13 +9,14 @@
 
 WINDOW_PATH = ((0, 0), (1, 0), (2, 0), (2, 1), (3, 1), (4, 1), (4, 2))
 STEP_ORDER = (1, 2, 5, 4, 3, 6)
+SEND_ORDER = (3, 4, 6, 5, 2, 1)
 MESH = pl.DeviceIdType.MESH
 
 
-def kernel(inner_count, outer_count, q_hbm, k_hbm, v_hbm, do_hbm, o_hbm, lse_ref, span_ref, code_ref,
-           dq_ref, dk_ref, dv_ref,
-           q_vm, do_vm, o_vm, kv_own, kv_in, g_out, g_in, dq_acc, own_acc,
-           load_sem, kv_send, kv_recv, g_send, g_recv):
+def kernel(inner_count, outer_count, q_hbm, k_hbm, v_hbm, do_hbm, o_hbm, lse_hbm, span_hbm, code_hbm,
+           dq_hbm, dk_hbm, dv_hbm,
+           lse_ref, span_ref, code_ref, dq_ref, sum_ref, q_vm, do_vm, o_vm, kv_own, kv_in, g_out, g_in, dq_acc, own_acc,
+           load_sem, store_sem, kv_send, kv_recv, g_send, g_recv):
     inner_at = lax.axis_index("inner")
     outer_at = lax.axis_index("outer")
     head_count, rows, width = q_vm.shape
@@ -30,9 +31,8 @@
         return u, w
 
     barrier = pltpu.get_barrier_semaphore()
-    for step in steps:
-        for sign in (1, -1):
-            pl.semaphore_signal(barrier, inc=1, device_id=device(step, sign), device_id_type=MESH)
+    for step in SEND_ORDER:
+        pl.semaphore_signal(barrier, inc=1, device_id=device(step, -1), device_id_type=MESH)
 
     loads = []
 
@@ -43,15 +43,18 @@
 
     load(k_hbm, kv_own.at[0], 0)
     load(v_hbm, kv_own.at[1], 1)
+    load(lse_hbm, lse_ref, 2 + 3 * head_count)
+    load(span_hbm, span_ref, 3 + 3 * head_count)
+    load(code_hbm, code_ref, 4 + 3 * head_count)
     for h in range(head_count):
         columns = pl.ds(h * width, width)
         load(q_hbm.at[:, columns], q_vm.at[h], 2 + 3 * h)
         load(do_hbm.at[:, columns], do_vm.at[h], 3 + 3 * h)
         load(o_hbm.at[:, columns], o_vm.at[h], 4 + 3 * h)
-    for copy in loads:
+    for copy in loads[:2]:
         copy.wait()
 
-    pl.semaphore_wait(barrier, 2 * len(steps))
+    pl.semaphore_wait(barrier, len(steps))
 
     def kv_copy(step):
         return pltpu.make_async_remote_copy(
@@ -65,8 +68,10 @@
             send_sem=g_send.at[step - 1], recv_sem=g_recv.at[step - 1],
             device_id=device(step, -1), device_id_type=MESH)
 
-    for step in STEP_ORDER:
+    for step in SEND_ORDER:
         kv_copy(step).start()
+    for copy in loads[2:]:
+        copy.wait()
 
     def spans(step):
         u, w = device(step, -1)
@@ -121,15 +126,33 @@
     for h in range(head_count):
         columns = pl.ds(h * rows, rows)
         dq_ref[:, pl.ds(h * width, width)] = dq_acc[:, columns].T.astype(jnp.bfloat16)
+    dq_store = pltpu.make_async_copy(dq_ref, dq_hbm, store_sem.at[0])
+    dq_store.start()
     total = own_acc[...]
     for step in STEP_ORDER:
         g_copy(step).wait_recv()
         total = total + g_in[step - 1].astype(jnp.float32)
-    dk_ref[...] = total[0].astype(jnp.bfloat16)
-    dv_ref[...] = total[1].astype(jnp.bfloat16)
+    sum_ref[...] = total.astype(jnp.bfloat16)
+    dk_store = pltpu.make_async_copy(sum_ref.at[0], dk_hbm, store_sem.at[1])
+    dv_store = pltpu.make_async_copy(sum_ref.at[1], dv_hbm, store_sem.at[2])
+    dk_store.start()
+    dv_store.start()
+    dq_store.wait()
+    dk_store.wait()
+    dv_store.wait()
     for step in STEP_ORDER:
         kv_copy(step).wait_send()
         g_copy(step).wait_send()
+
+
+def finish(dq_in, dk_in, dv_in, dq_out, dk_out, dv_out, sem):
+    moves = []
+    for slot, (src, dst) in enumerate(((dq_in, dq_out), (dk_in, dk_out), (dv_in, dv_out))):
+        move = pltpu.make_async_copy(src, dst, sem.at[slot])
+        move.start()
+        moves.append(move)
+    for move in moves:
+        move.wait()
 
 
 def shards(queries, keys, values, out_grad, forward_out, log_sum_exp, span_table, mask_codes):
@@ -139,17 +162,22 @@
     remote = len(WINDOW_PATH) - 1
     hbm = pl.BlockSpec(memory_space=pl.ANY)
     vmem = pl.BlockSpec(memory_space=pltpu.VMEM)
-    smem = pl.BlockSpec(memory_space=pltpu.SMEM)
-    return pl.pallas_call(
+    grads = (
+        jax.ShapeDtypeStruct((rows, features), jnp.bfloat16),
+        jax.ShapeDtypeStruct((rows, width), jnp.bfloat16),
+        jax.ShapeDtypeStruct((rows, width), jnp.bfloat16),
+    )
+    parts = pl.pallas_call(
         functools.partial(kernel, lax.axis_size("inner"), lax.axis_size("outer")),
-        out_shape=(
-            jax.ShapeDtypeStruct((rows, features), jnp.bfloat16),
-            jax.ShapeDtypeStruct((rows, width), jnp.bfloat16),
-            jax.ShapeDtypeStruct((rows, width), jnp.bfloat16),
-        ),
-        in_specs=[hbm, hbm, hbm, hbm, hbm, vmem, smem, smem],
-        out_specs=(vmem, vmem, vmem),
+        out_shape=grads,
+        in_specs=[hbm] * 8,
+        out_specs=(hbm, hbm, hbm),
         scratch_shapes=[
+            pltpu.VMEM((heads, rows), jnp.float32),
+            pltpu.SMEM(span_table.shape, jnp.int32),
+            pltpu.SMEM(mask_codes.shape, jnp.int32),
+            pltpu.VMEM((rows, features), jnp.bfloat16),
+            pltpu.VMEM((2, rows, width), jnp.bfloat16),
             pltpu.VMEM((heads, rows, width), jnp.bfloat16),
             pltpu.VMEM((heads, rows, width), jnp.bfloat16),
             pltpu.VMEM((heads, rows, width), jnp.bfloat16),
@@ -159,14 +187,24 @@
             pltpu.VMEM((remote, 2, rows, width), jnp.bfloat16),
             pltpu.VMEM((width, heads * rows), jnp.float32),
             pltpu.VMEM((2, rows, width), jnp.float32),
-            pltpu.SemaphoreType.DMA((2 + 3 * heads,)),
+            pltpu.SemaphoreType.DMA((5 + 3 * heads,)),
+            pltpu.SemaphoreType.DMA((3,)),
             pltpu.SemaphoreType.DMA((remote,)),
             pltpu.SemaphoreType.DMA((remote,)),
             pltpu.SemaphoreType.DMA((remote,)),
             pltpu.SemaphoreType.DMA((remote,)),
         ],
-        compiler_params=pltpu.CompilerParams(collective_id=0, has_side_effects=True),
+        compiler_params=pltpu.CompilerParams(
+            collective_id=0, has_side_effects=True),
     )(queries, keys, values, out_grad, forward_out, log_sum_exp, span_table, mask_codes)
+    return pl.pallas_call(
+        finish,
+        out_shape=grads,
+        in_specs=[vmem] * 3,
+        out_specs=(hbm, hbm, hbm),
+        scratch_shapes=[pltpu.SemaphoreType.DMA((3,))],
+        compiler_params=pltpu.CompilerParams(vmem_limit_bytes=16 * 2 ** 20),
+    )(*parts)
 
 
 def solution(mesh):

time: 25 us -> 25.1 us (level)
  Pallas kernels: 21 us -> 21.6 us
  local copies, waits for them, and re-layouts: 3.06 us -> 2.46 us
    pallas_call x0 -> x1, Pallas kernels: none -> 0.74 us  [shards(): pl.pallas_call(finish, out_shape=grads, in_specs=[vmem] * 3, out_specs=(h...]
    unnamed x7 -> x6, local copies, waits for them, and re-layouts: 3.06 us -> 2.46 us
where the time goes in v2:
time: 25.1 us; the launch traced here: 24.7 us
  Pallas kernels  21.6 us (86%)
  local copies, waits for them, and re-layouts  2.46 us (10%)
  between operations  0.65 us (3%)
    pallas_call x1, Pallas kernels, shards(): pl.pallas_call(functools.partial(kernel, lax.axis_size('inner'), lax.axis...  20.9 us
    unnamed x6, local copies, waits for them, and re-layouts  2.46 us
    pallas_call x1, Pallas kernels, shards(): pl.pallas_call(finish, out_shape=grads, in_specs=[vmem] * 3, out_specs=(h...  0.74 us

profile of v2, /device:TPU:0, one launch (start us, length us, event | category | flops | bytes accessed | tf_op | source)
XLA Modules:
  0.0 24.7 jit_solution(5420135406397872459)
XLA Ops:
  0.6 20.9 %shard_map.103 = (bf16[128,1024]{1,0:T(8,128)(2,1)}, bf16[128,128]{1,0:T(8,128)(2,1)}, bf16[128,128]{1,0:T(8,128)(2,1)}) custom-call(bf16[128,1024]{1,0:T(8,128)(2,1)} %q_hbm.1, bf16[128,128]{1,0:T(8,128)(2,1)} %k_hbm.1, bf16[128,128]{1,0:T(8,128)(2,1)} %v_hbm.1, bf16[128,1024]{1,0:T(8,128)(2,1)} %do_hbm.1, bf16[128,1024]{1,0:T(8,128)(2,1)} %o_hbm.1, ...), custom_call_target="tpu_custom_call" | custom-call | tf_op jit(solution)/shard_map/pallas_call | solution.py:170
  21.5 0.0 copy-start
  21.5 0.9 %copy-done = bf16[128,1024]{1,0:T(8,128)(2,1)S(1)} copy-done((bf16[128,1024]{1,0:T(8,128)(2,1)S(1)}, bf16[128,1024]{1,0:T(8,128)(2,1)}, u32[]{:S(2)}) %copy-start) | copy-done | bytes 262168
  22.5 0.0 copy-start.1
  22.5 0.8 %copy-done.1 = bf16[128,128]{1,0:T(8,128)(2,1)S(1)} copy-done((bf16[128,128]{1,0:T(8,128)(2,1)S(1)}, bf16[128,128]{1,0:T(8,128)(2,1)}, u32[]{:S(2)}) %copy-start.1) | copy-done | bytes 32792
  23.2 0.0 copy-start.2
  23.2 0.8 %copy-done.2 = bf16[128,128]{1,0:T(8,128)(2,1)S(1)} copy-done((bf16[128,128]{1,0:T(8,128)(2,1)S(1)}, bf16[128,128]{1,0:T(8,128)(2,1)}, u32[]{:S(2)}) %copy-start.2) | copy-done | bytes 32792
  24.0 0.7 %shard_map.104 = (bf16[128,1024]{1,0:T(8,128)(2,1)}, bf16[128,128]{1,0:T(8,128)(2,1)}, bf16[128,128]{1,0:T(8,128)(2,1)}) custom-call(bf16[128,1024]{1,0:T(8,128)(2,1)S(1)} %copy-done, bf16[128,128]{1,0:T(8,128)(2,1)S(1)} %copy-done.1, bf16[128,128]{1,0:T(8,128)(2,1)S(1)} %copy-done.2), custom_call_target="tpu_custom_call" | custom-call | tf_op jit(solution)/shard_map/pallas_call | solution.py:200
Async XLA Ops:
  21.5 1.0 %copy-start = (bf16[128,1024]{1,0:T(8,128)(2,1)S(1)}, bf16[128,1024]{1,0:T(8,128)(2,1)}, u32[]{:S(2)}) copy-start(bf16[128,1024]{1,0:T(8,128)(2,1)} %get-tuple-element.6.dq_in) | copy-start | bytes 786436
  22.5 0.8 %copy-start.1 = (bf16[128,128]{1,0:T(8,128)(2,1)S(1)}, bf16[128,128]{1,0:T(8,128)(2,1)}, u32[]{:S(2)}) copy-start(bf16[128,128]{1,0:T(8,128)(2,1)} %get-tuple-element.7.dk_in) | copy-start | bytes 98308
  23.2 0.8 %copy-start.2 = (bf16[128,128]{1,0:T(8,128)(2,1)S(1)}, bf16[128,128]{1,0:T(8,128)(2,1)}, u32[]{:S(2)}) copy-start(bf16[128,128]{1,0:T(8,128)(2,1)} %get-tuple-element.8.dv_in) | copy-start | bytes 98308

commit v3 on v2

--- a/solution.py
+++ b/solution.py
@@ -9,13 +9,15 @@
 
 WINDOW_PATH = ((0, 0), (1, 0), (2, 0), (2, 1), (3, 1), (4, 1), (4, 2))
 STEP_ORDER = (1, 2, 5, 4, 3, 6)
-SEND_ORDER = (3, 4, 6, 5, 2, 1)
+DIRECT = (5, 6, 2, 1)
+HUB = 5
+RELAYED = (3, 4)
 MESH = pl.DeviceIdType.MESH
 
 
 def kernel(inner_count, outer_count, q_hbm, k_hbm, v_hbm, do_hbm, o_hbm, lse_hbm, span_hbm, code_hbm,
            dq_hbm, dk_hbm, dv_hbm,
-           lse_ref, span_ref, code_ref, dq_ref, sum_ref, q_vm, do_vm, o_vm, kv_own, kv_in, g_out, g_in, dq_acc, own_acc,
+           lse_ref, span_ref, code_ref, dq_ref, sum_ref, q_vm, do_vm, o_vm, kv_own, kv_in, g_out, g_in, dq_acc, own_acc, hub_acc,
            load_sem, store_sem, kv_send, kv_recv, g_send, g_recv):
     inner_at = lax.axis_index("inner")
     outer_at = lax.axis_index("outer")
@@ -24,15 +26,30 @@
     scale = width ** (-0.5)
     steps = range(1, len(WINDOW_PATH))
 
+    def shifted(a, c):
+        u = lax.rem(inner_at + a % inner_count, inner_count)
+        w = lax.rem(outer_at + c % outer_count, outer_count)
+        return u, w
+
     def device(step, sign):
         a, c = WINDOW_PATH[step]
-        u = lax.rem(inner_at + (sign * a) % inner_count, inner_count)
-        w = lax.rem(outer_at + (sign * c) % outer_count, outer_count)
-        return u, w
+        return shifted(sign * a, sign * c)
+
+    def reader(step):
+        a, c = WINDOW_PATH[step]
+        if step in RELAYED:
+            return shifted(a - WINDOW_PATH[HUB][0], c - WINDOW_PATH[HUB][1])
+        return shifted(a, c)
+
+    def sender(step):
+        a, c = WINDOW_PATH[step]
+        if step in RELAYED:
+            return shifted(WINDOW_PATH[HUB][0] - a, WINDOW_PATH[HUB][1] - c)
+        return shifted(-a, -c)
 
     barrier = pltpu.get_barrier_semaphore()
-    for step in SEND_ORDER:
-        pl.semaphore_signal(barrier, inc=1, device_id=device(step, -1), device_id_type=MESH)
+    for step in DIRECT + RELAYED:
+        pl.semaphore_signal(barrier, inc=1, device_id=sender(step), device_id_type=MESH)
 
     loads = []
 
@@ -56,20 +73,22 @@
 
     pl.semaphore_wait(barrier, len(steps))
 
-    def kv_copy(step):
+    def kv_copy(step, part):
+        source = kv_in.at[HUB - 1, part] if step in RELAYED else kv_own.at[part]
         return pltpu.make_async_remote_copy(
-            src_ref=kv_own, dst_ref=kv_in.at[step - 1],
-            send_sem=kv_send.at[step - 1], recv_sem=kv_recv.at[step - 1],
-            device_id=device(step, 1), device_id_type=MESH)
-
-    def g_copy(step):
+            src_ref=source, dst_ref=kv_in.at[step - 1, part],
+            send_sem=kv_send.at[step - 1, part], recv_sem=kv_recv.at[step - 1, part],
+            device_id=reader(step), device_id_type=MESH)
+
+    def g_copy(step, part):
         return pltpu.make_async_remote_copy(
-            src_ref=g_out.at[step - 1], dst_ref=g_in.at[step - 1],
-            send_sem=g_send.at[step - 1], recv_sem=g_recv.at[step - 1],
-            device_id=device(step, -1), device_id_type=MESH)
-
-    for step in SEND_ORDER:
-        kv_copy(step).start()
+            src_ref=g_out.at[step - 1, part], dst_ref=g_in.at[step - 1, part],
+            send_sem=g_send.at[step - 1, part], recv_sem=g_recv.at[step - 1, part],
+            device_id=sender(step), device_id_type=MESH)
+
+    for step in DIRECT:
+        for part in range(2):
+            kv_copy(step, part).start()
     for copy in loads[2:]:
         copy.wait()
 
@@ -116,23 +135,41 @@
         return query_part, key_part, value_part
 
     dq_acc[...], own_acc[0], own_acc[1] = visit(0, kv_own[0], kv_own[1])
+    def put(step, part, value):
+        g_out[step - 1, part] = value.astype(jnp.bfloat16)
+        g_copy(step, part).start()
+
     for step in STEP_ORDER:
-        kv_copy(step).wait_recv()
+        for part in range(2):
+            kv_copy(step, part).wait_recv()
+            if step == HUB:
+                for onward in RELAYED:
+                    kv_copy(onward, part).start()
         query_part, key_part, value_part = visit(step, kv_in[step - 1, 0], kv_in[step - 1, 1])
-        g_out[step - 1, 0] = key_part.astype(jnp.bfloat16)
-        g_out[step - 1, 1] = value_part.astype(jnp.bfloat16)
-        g_copy(step).start()
+        if step == HUB:
+            hub_acc[0] = key_part
+            hub_acc[1] = value_part
+        else:
+            put(step, 1, value_part)
+            put(step, 0, key_part)
         dq_acc[...] += query_part
     for h in range(head_count):
         columns = pl.ds(h * rows, rows)
         dq_ref[:, pl.ds(h * width, width)] = dq_acc[:, columns].T.astype(jnp.bfloat16)
     dq_store = pltpu.make_async_copy(dq_ref, dq_hbm, store_sem.at[0])
     dq_store.start()
-    total = own_acc[...]
-    for step in STEP_ORDER:
-        g_copy(step).wait_recv()
-        total = total + g_in[step - 1].astype(jnp.float32)
-    sum_ref[...] = total.astype(jnp.bfloat16)
+    for part in (1, 0):
+        joined = hub_acc[part]
+        for step in RELAYED:
+            g_copy(step, part).wait_recv()
+            joined = joined + g_in[step - 1, part].astype(jnp.float32)
+        put(HUB, part, joined)
+    for part in (1, 0):
+        total = own_acc[part]
+        for step in (1, 2, 6, HUB):
+            g_copy(step, part).wait_recv()
+            total = total + g_in[step - 1, part].astype(jnp.float32)
+        sum_ref[part] = total.astype(jnp.bfloat16)
     dk_store = pltpu.make_async_copy(sum_ref.at[0], dk_hbm, store_sem.at[1])
     dv_store = pltpu.make_async_copy(sum_ref.at[1], dv_hbm, store_sem.at[2])
     dk_store.start()
@@ -141,18 +178,26 @@
     dk_store.wait()
     dv_store.wait()
     for step in STEP_ORDER:
-        kv_copy(step).wait_send()
-        g_copy(step).wait_send()
-
-
-def finish(dq_in, dk_in, dv_in, dq_out, dk_out, dv_out, sem):
+        for part in range(2):
+            kv_copy(step, part).wait_send()
+            g_copy(step, part).wait_send()
+
+
+def finish(dq_in, dk_in, dv_in, dq_out, dk_out, dv_out, dq_vm, dk_vm, dv_vm, in_sem, out_sem):
     moves = []
-    for slot, (src, dst) in enumerate(((dq_in, dq_out), (dk_in, dk_out), (dv_in, dv_out))):
-        move = pltpu.make_async_copy(src, dst, sem.at[slot])
-        move.start()
-        moves.append(move)
-    for move in moves:
-        move.wait()
+    rows = dq_vm.shape[0]
+    quarter = rows // 4
+    pieces = [(dq_in, dq_vm, dq_out, pl.ds(at * quarter, quarter)) for at in range(4)]
+    pieces += [(dk_in, dk_vm, dk_out, pl.ds(0, rows)), (dv_in, dv_vm, dv_out, pl.ds(0, rows))]
+    for slot, (src, held, dst, part) in enumerate(pieces):
+        get = pltpu.make_async_copy(src.at[part], held.at[part], in_sem.at[slot])
+        get.start()
+        moves.append((get, pltpu.make_async_copy(held.at[part], dst.at[part], out_sem.at[slot])))
+    for get, out in moves:
+        get.wait()
+        out.start()
+    for _, out in moves:
+        out.wait()
 
 
 def shards(queries, keys, values, out_grad, forward_out, log_sum_exp, span_table, mask_codes):
@@ -161,7 +206,6 @@
     heads = log_sum_exp.shape[0]
     remote = len(WINDOW_PATH) - 1
     hbm = pl.BlockSpec(memory_space=pl.ANY)
-    vmem = pl.BlockSpec(memory_space=pltpu.VMEM)
     grads = (
         jax.ShapeDtypeStruct((rows, features), jnp.bfloat16),
         jax.ShapeDtypeStruct((rows, width), jnp.bfloat16),
@@ -187,12 +231,13 @@
             pltpu.VMEM((remote, 2, rows, width), jnp.bfloat16),
             pltpu.VMEM((width, heads * rows), jnp.float32),
             pltpu.VMEM((2, rows, width), jnp.float32),
+            pltpu.VMEM((2, rows, width), jnp.float32),
             pltpu.SemaphoreType.DMA((5 + 3 * heads,)),
             pltpu.SemaphoreType.DMA((3,)),
-            pltpu.SemaphoreType.DMA((remote,)),
-            pltpu.SemaphoreType.DMA((remote,)),
-            pltpu.SemaphoreType.DMA((remote,)),
-            pltpu.SemaphoreType.DMA((remote,)),
+            pltpu.SemaphoreType.DMA((remote, 2)),
+            pltpu.SemaphoreType.DMA((remote, 2)),
+            pltpu.SemaphoreType.DMA((remote, 2)),
+            pltpu.SemaphoreType.DMA((remote, 2)),
         ],
         compiler_params=pltpu.CompilerParams(
             collective_id=0, has_side_effects=True),
@@ -200,10 +245,10 @@
     return pl.pallas_call(
         finish,
         out_shape=grads,
-        in_specs=[vmem] * 3,
+        in_specs=[hbm] * 3,
         out_specs=(hbm, hbm, hbm),
-        scratch_shapes=[pltpu.SemaphoreType.DMA((3,))],
-        compiler_params=pltpu.CompilerParams(vmem_limit_bytes=16 * 2 ** 20),
+        scratch_shapes=[pltpu.VMEM(grad.shape, grad.dtype) for grad in grads]
+        + [pltpu.SemaphoreType.DMA((6,)), pltpu.SemaphoreType.DMA((6,))],
     )(*parts)
 
 

time: 25.1 us -> 23.9 us (0.952)
  local copies, waits for them, and re-layouts: 2.46 us -> 0 us
  Pallas kernels: 21.6 us -> 23 us
    unnamed x6 -> x0, local copies, waits for them, and re-layouts: 2.46 us -> none
    pallas_call x1, Pallas kernels: 0.74 us -> 1.69 us  [shards(): pl.pallas_call(finish, out_shape=grads, in_specs=[hbm] * 3, out_specs=(hb...]
    pallas_call x1, Pallas kernels: 20.9 us -> 21.4 us  [shards(): pl.pallas_call(functools.partial(kernel, lax.axis_size('inner'), lax.axis...]
where the time goes in v3:
time: 23.9 us; the launch traced here: 23.7 us
  Pallas kernels  23 us (96%)
  between operations  0.64 us (3%)
    pallas_call x1, Pallas kernels, shards(): pl.pallas_call(functools.partial(kernel, lax.axis_size('inner'), lax.axis...  21.4 us
    pallas_call x1, Pallas kernels, shards(): pl.pallas_call(finish, out_shape=grads, in_specs=[hbm] * 3, out_specs=(hb...  1.69 us

profile of v3, /device:TPU:0, one launch (start us, length us, event | category | flops | bytes accessed | tf_op | source)
XLA Modules:
  0.0 23.7 jit_solution(1986302787726821803)
XLA Ops:
  0.6 21.4 %shard_map.103 = (bf16[128,1024]{1,0:T(8,128)(2,1)}, bf16[128,128]{1,0:T(8,128)(2,1)}, bf16[128,128]{1,0:T(8,128)(2,1)}) custom-call(bf16[128,1024]{1,0:T(8,128)(2,1)} %q_hbm.1, bf16[128,128]{1,0:T(8,128)(2,1)} %k_hbm.1, bf16[128,128]{1,0:T(8,128)(2,1)} %v_hbm.1, bf16[128,1024]{1,0:T(8,128)(2,1)} %do_hbm.1, bf16[128,1024]{1,0:T(8,128)(2,1)} %o_hbm.1, ...), custom_call_target="tpu_custom_call" | custom-call | tf_op jit(solution)/shard_map/pallas_call | solution.py:214
  22.0 1.7 %shard_map.104 = (bf16[128,1024]{1,0:T(8,128)(2,1)}, bf16[128,128]{1,0:T(8,128)(2,1)}, bf16[128,128]{1,0:T(8,128)(2,1)}) custom-call(bf16[128,1024]{1,0:T(8,128)(2,1)} %get-tuple-element.6.dq_in, bf16[128,128]{1,0:T(8,128)(2,1)} %get-tuple-element.7.dk_in, bf16[128,128]{1,0:T(8,128)(2,1)} %get-tuple-element.8.dv_in), custom_call_target="tpu_custom_call" | custom-call | tf_op jit(solution)/shard_map/pallas_call | solution.py:245

commit v4 on v3

--- a/solution.py
+++ b/solution.py
@@ -9,15 +9,13 @@
 
 WINDOW_PATH = ((0, 0), (1, 0), (2, 0), (2, 1), (3, 1), (4, 1), (4, 2))
 STEP_ORDER = (1, 2, 5, 4, 3, 6)
-DIRECT = (5, 6, 2, 1)
-HUB = 5
-RELAYED = (3, 4)
+SEND_ORDER = (3, 4, 6, 5, 2, 1)
 MESH = pl.DeviceIdType.MESH
 
 
 def kernel(inner_count, outer_count, q_hbm, k_hbm, v_hbm, do_hbm, o_hbm, lse_hbm, span_hbm, code_hbm,
            dq_hbm, dk_hbm, dv_hbm,
-           lse_ref, span_ref, code_ref, dq_ref, sum_ref, q_vm, do_vm, o_vm, kv_own, kv_in, g_out, g_in, dq_acc, own_acc, hub_acc,
+           lse_ref, span_ref, code_ref, dq_ref, sum_ref, q_vm, do_vm, o_vm, kv_own, kv_in, g_out, g_in, dq_acc, own_acc,
            load_sem, store_sem, kv_send, kv_recv, g_send, g_recv):
     inner_at = lax.axis_index("inner")
     outer_at = lax.axis_index("outer")
@@ -35,21 +33,9 @@
         a, c = WINDOW_PATH[step]
         return shifted(sign * a, sign * c)
 
-    def reader(step):
-        a, c = WINDOW_PATH[step]
-        if step in RELAYED:
-            return shifted(a - WINDOW_PATH[HUB][0], c - WINDOW_PATH[HUB][1])
-        return shifted(a, c)
-
-    def sender(step):
-        a, c = WINDOW_PATH[step]
-        if step in RELAYED:
-            return shifted(WINDOW_PATH[HUB][0] - a, WINDOW_PATH[HUB][1] - c)
-        return shifted(-a, -c)
-
     barrier = pltpu.get_barrier_semaphore()
-    for step in DIRECT + RELAYED:
-        pl.semaphore_signal(barrier, inc=1, device_id=sender(step), device_id_type=MESH)
+    for step in SEND_ORDER:
+        pl.semaphore_signal(barrier, inc=1, device_id=device(step, -1), device_id_type=MESH)
 
     loads = []
 
@@ -74,19 +60,18 @@
     pl.semaphore_wait(barrier, len(steps))
 
     def kv_copy(step, part):
-        source = kv_in.at[HUB - 1, part] if step in RELAYED else kv_own.at[part]
         return pltpu.make_async_remote_copy(
-            src_ref=source, dst_ref=kv_in.at[step - 1, part],
+            src_ref=kv_own.at[part], dst_ref=kv_in.at[step - 1, part],
             send_sem=kv_send.at[step - 1, part], recv_sem=kv_recv.at[step - 1, part],
-            device_id=reader(step), device_id_type=MESH)
+            device_id=device(step, 1), device_id_type=MESH)
 
     def g_copy(step, part):
         return pltpu.make_async_remote_copy(
             src_ref=g_out.at[step - 1, part], dst_ref=g_in.at[step - 1, part],
             send_sem=g_send.at[step - 1, part], recv_sem=g_recv.at[step - 1, part],
-            device_id=sender(step), device_id_type=MESH)
-
-    for step in DIRECT:
+            device_id=device(step, -1), device_id_type=MESH)
+
+    for step in SEND_ORDER:
         for part in range(2):
             kv_copy(step, part).start()
     for copy in loads[2:]:
@@ -142,16 +127,9 @@
     for step in STEP_ORDER:
         for part in range(2):
             kv_copy(step, part).wait_recv()
-            if step == HUB:
-                for onward in RELAYED:
-                    kv_copy(onward, part).start()
         query_part, key_part, value_part = visit(step, kv_in[step - 1, 0], kv_in[step - 1, 1])
-        if step == HUB:
-            hub_acc[0] = key_part
-            hub_acc[1] = value_part
-        else:
-            put(step, 1, value_part)
-            put(step, 0, key_part)
+        put(step, 1, value_part)
+        put(step, 0, key_part)
         dq_acc[...] += query_part
     for h in range(head_count):
         columns = pl.ds(h * rows, rows)
@@ -159,14 +137,8 @@
     dq_store = pltpu.make_async_copy(dq_ref, dq_hbm, store_sem.at[0])
     dq_store.start()
     for part in (1, 0):
-        joined = hub_acc[part]
-        for step in RELAYED:
-            g_copy(step, part).wait_recv()
-            joined = joined + g_in[step - 1, part].astype(jnp.float32)
-        put(HUB, part, joined)
-    for part in (1, 0):
         total = own_acc[part]
-        for step in (1, 2, 6, HUB):
+        for step in STEP_ORDER:
             g_copy(step, part).wait_recv()
             total = total + g_in[step - 1, part].astype(jnp.float32)
         sum_ref[part] = total.astype(jnp.bfloat16)
@@ -231,7 +203,6 @@
             pltpu.VMEM((remote, 2, rows, width), jnp.bfloat16),
             pltpu.VMEM((width, heads * rows), jnp.float32),
             pltpu.VMEM((2, rows, width), jnp.float32),
-            pltpu.VMEM((2, rows, width), jnp.float32),
             pltpu.SemaphoreType.DMA((5 + 3 * heads,)),
             pltpu.SemaphoreType.DMA((3,)),
             pltpu.SemaphoreType.DMA((remote, 2)),

time: 23.9 us -> 23.6 us (0.987)
  Pallas kernels: 23 us -> 22.7 us
    pallas_call x1, Pallas kernels: 21.4 us -> 21 us  [shards(): pl.pallas_call(functools.partial(kernel, lax.axis_size('inner'), lax.axis...]
where the time goes in v4:
time: 23.6 us; the launch traced here: 23.3 us
  Pallas kernels  22.7 us (96%)
  between operations  0.64 us (3%)
    pallas_call x1, Pallas kernels, shards(): pl.pallas_call(functools.partial(kernel, lax.axis_size('inner'), lax.axis...  21 us
    pallas_call x1, Pallas kernels, shards(): pl.pallas_call(finish, out_shape=grads, in_specs=[hbm] * 3, out_specs=(hb...  1.69 us

profile of v4, /device:TPU:0, one launch (start us, length us, event | category | flops | bytes accessed | tf_op | source)
XLA Modules:
  0.0 23.3 jit_solution(4463610328579917773)
XLA Ops:
  0.6 21.0 %shard_map.103 = (bf16[128,1024]{1,0:T(8,128)(2,1)}, bf16[128,128]{1,0:T(8,128)(2,1)}, bf16[128,128]{1,0:T(8,128)(2,1)}) custom-call(bf16[128,1024]{1,0:T(8,128)(2,1)} %q_hbm.1, bf16[128,128]{1,0:T(8,128)(2,1)} %k_hbm.1, bf16[128,128]{1,0:T(8,128)(2,1)} %v_hbm.1, bf16[128,1024]{1,0:T(8,128)(2,1)} %do_hbm.1, bf16[128,1024]{1,0:T(8,128)(2,1)} %o_hbm.1, ...), custom_call_target="tpu_custom_call" | custom-call | tf_op jit(solution)/shard_map/pallas_call | solution.py:186
  21.7 1.7 %shard_map.104 = (bf16[128,1024]{1,0:T(8,128)(2,1)}, bf16[128,128]{1,0:T(8,128)(2,1)}, bf16[128,128]{1,0:T(8,128)(2,1)}) custom-call(bf16[128,1024]{1,0:T(8,128)(2,1)} %get-tuple-element.6.dq_in, bf16[128,128]{1,0:T(8,128)(2,1)} %get-tuple-element.7.dk_in, bf16[128,128]{1,0:T(8,128)(2,1)} %get-tuple-element.8.dv_in), custom_call_target="tpu_custom_call" | custom-call | tf_op jit(solution)/shard_map/pallas_call | solution.py:216

commit v5 on v4

--- a/solution.py
+++ b/solution.py
@@ -8,7 +8,7 @@
 from jax.sharding import PartitionSpec as P
 
 WINDOW_PATH = ((0, 0), (1, 0), (2, 0), (2, 1), (3, 1), (4, 1), (4, 2))
-STEP_ORDER = (1, 2, 5, 4, 3, 6)
+STEP_ORDER = (1, 2, 6, 5, 4, 3)
 SEND_ORDER = (3, 4, 6, 5, 2, 1)
 MESH = pl.DeviceIdType.MESH
 
@@ -136,16 +136,15 @@
         dq_ref[:, pl.ds(h * width, width)] = dq_acc[:, columns].T.astype(jnp.bfloat16)
     dq_store = pltpu.make_async_copy(dq_ref, dq_hbm, store_sem.at[0])
     dq_store.start()
-    for part in (1, 0):
+    dk_store = pltpu.make_async_copy(sum_ref.at[0], dk_hbm, store_sem.at[1])
+    dv_store = pltpu.make_async_copy(sum_ref.at[1], dv_hbm, store_sem.at[2])
+    for part, store in ((1, dv_store), (0, dk_store)):
         total = own_acc[part]
         for step in STEP_ORDER:
             g_copy(step, part).wait_recv()
             total = total + g_in[step - 1, part].astype(jnp.float32)
         sum_ref[part] = total.astype(jnp.bfloat16)
-    dk_store = pltpu.make_async_copy(sum_ref.at[0], dk_hbm, store_sem.at[1])
-    dv_store = pltpu.make_async_copy(sum_ref.at[1], dv_hbm, store_sem.at[2])
-    dk_store.start()
-    dv_store.start()
+        store.start()
     dq_store.wait()
     dk_store.wait()
     dv_store.wait()

time: 23.6 us -> 22.2 us (0.941)
  Pallas kernels: 22.7 us -> 21.3 us
    pallas_call x1, Pallas kernels: 21 us -> 19.6 us  [shards(): pl.pallas_call(functools.partial(kernel, lax.axis_size('inner'), lax.axis...]
where the time goes in v5:
time: 22.2 us; the launch traced here: 21.9 us
  Pallas kernels  21.3 us (96%)
  between operations  0.64 us (3%)
    pallas_call x1, Pallas kernels, shards(): pl.pallas_call(functools.partial(kernel, lax.axis_size('inner'), lax.axis...  19.6 us
    pallas_call x1, Pallas kernels, shards(): pl.pallas_call(finish, out_shape=grads, in_specs=[hbm] * 3, out_specs=(hb...  1.69 us

profile of v5, /device:TPU:0, one launch (start us, length us, event | category | flops | bytes accessed | tf_op | source)
XLA Modules:
  0.0 21.9 jit_solution(1131394470373614735)
XLA Ops:
  0.6 19.6 %shard_map.103 = (bf16[128,1024]{1,0:T(8,128)(2,1)}, bf16[128,128]{1,0:T(8,128)(2,1)}, bf16[128,128]{1,0:T(8,128)(2,1)}) custom-call(bf16[128,1024]{1,0:T(8,128)(2,1)} %q_hbm.1, bf16[128,128]{1,0:T(8,128)(2,1)} %k_hbm.1, bf16[128,128]{1,0:T(8,128)(2,1)} %v_hbm.1, bf16[128,1024]{1,0:T(8,128)(2,1)} %do_hbm.1, bf16[128,1024]{1,0:T(8,128)(2,1)} %o_hbm.1, ...), custom_call_target="tpu_custom_call" | custom-call | tf_op jit(solution)/shard_map/pallas_call | solution.py:185
  20.2 1.7 %shard_map.104 = (bf16[128,1024]{1,0:T(8,128)(2,1)}, bf16[128,128]{1,0:T(8,128)(2,1)}, bf16[128,128]{1,0:T(8,128)(2,1)}) custom-call(bf16[128,1024]{1,0:T(8,128)(2,1)} %get-tuple-element.6.dq_in, bf16[128,128]{1,0:T(8,128)(2,1)} %get-tuple-element.7.dk_in, bf16[128,128]{1,0:T(8,128)(2,1)} %get-tuple-element.8.dv_in), custom_call_target="tpu_custom_call" | custom-call | tf_op jit(solution)/shard_map/pallas_call | solution.py:215
